TPU v7x, 512 devices: a whole 4x4x16 slice. The times are simulated.
512 devices in a mesh: rows: 32 (over x, y, core), upd: 16 (over z).
Axes of the slice: x: 4, y: 4, z: 16, core: 2. Of those that a mesh axis runs over, the one named last changes fastest.
Arguments:
- tile_factors: bfloat16 [32, 128, 1024, 128], P('rows', 'upd'), may hold values from -6 to 6
- panel_factors: bfloat16 [128, 1024, 128], P('upd', 'rows'), may hold values from -0.1875 to 0.1875
- nonnull: int32 [32, 128], P('rows', 'upd'), may hold values from 0 to 1, as said below
- sketch: float32 [64, 1024], replicated, may hold values from -6 to 6
Outputs:
- update_factors: float32 [32, 1024, 128], P('rows', 'upd')
Inputs may be any that keep to these rules, and one draw needn't show every extreme that they name: In every aligned block of 8 update indices the first one is nonnull for every tile row.
All inputs are finite; a program needn't handle non-finite values.
Results may differ from a plain program's by a relative error of at most 0.0003.
Values may be sent and summed in bfloat16 or wider, within the bound.
No kernel may reach another device: no remote copies, remote signals or barrier semaphores. Data moves between devices by JAX's collectives and lax.ppermute only.
A program may use at most 64 MiB of HBM per device.

v0:
```python
import jax
import jax.numpy as jnp
from jax import lax
from jax.sharding import PartitionSpec as P


def from_partner(shard, axis, stride):
    return lax.ppermute(shard, axis, [(i, i ^ 1 << stride) for i in range(lax.axis_size(axis))])


def compress(lefts, rights, sketch):
    hi = lax.Precision.HIGHEST
    proj = jnp.einsum("nbr,sb->nrs", rights, sketch, precision=hi)
    span = jnp.einsum("nbr,nrs->bs", lefts, proj, precision=hi)
    gram = jnp.dot(span.T, span, precision=hi)
    order = gram.shape[0]
    shift = 0.001 * jnp.trace(gram) / order + 1e-20
    gram = gram + shift * jnp.eye(order, dtype=gram.dtype)
    chol = jnp.linalg.cholesky(gram)
    basis = lax.linalg.triangular_solve(chol, span, left_side=False, lower=True, transpose_a=True)
    coef = jnp.einsum("nbr,bs->nrs", lefts, basis, precision=hi)
    image = jnp.einsum("nbr,nrs->bs", rights, coef, precision=hi)
    return (basis, image)


def merge_pair(pair, sketch, rank):
    basis, image = compress(pair[:, :, :rank], pair[:, :, rank:], sketch)
    return jnp.concatenate([basis, image], axis=-1)


def body(tile_factors, panel_factors, nonnull, sketch):
    rank = tile_factors.shape[3] // 2
    tiles = tile_factors[0]
    own_right = tiles[:, :, rank:]
    panel = lax.all_gather(panel_factors, "rows", axis=1, tiled=True)
    inner = jnp.einsum(
        "kbr,kbs->krs", own_right, panel[:, :, rank:], preferred_element_type=jnp.float32
    )
    far_left = panel[:, :, :rank]
    weight = nonnull[0].astype(jnp.float32)
    lefts = jnp.einsum(
        "kbr,krs->kbs",
        tiles[:, :, :rank].astype(jnp.float32),
        inner,
        precision=lax.Precision.HIGHEST,
    )
    lefts = lefts * weight[:, None, None]
    basis, image = compress(lefts, far_left.astype(jnp.float32), sketch)
    packed = jnp.concatenate([basis, image], axis=-1)
    levels = lax.axis_size("upd").bit_length() - 1
    for level in range(levels):
        other = from_partner(packed, "upd", level)
        upper = lax.axis_index("upd") >> level & 1 == 1
        low = jnp.where(upper, other, packed)
        high = jnp.where(upper, packed, other)
        packed = merge_pair(jnp.stack([low, high]), sketch, rank)
    scale = jnp.float32(packed.shape[0]) ** 0.5
    result = jnp.concatenate([packed[:, :rank] * scale, packed[:, rank:] / scale], axis=-1)
    share = packed.shape[0] // lax.axis_size("upd")
    mine = lax.dynamic_slice_in_dim(result, lax.axis_index("upd") * share, share, 0)
    return mine[None]


def solution(mesh):
    in_specs = (P("rows", "upd", None, None), P("upd", "rows", None), P("rows", "upd"), P())
    out_specs = P("rows", "upd", None)
    return jax.shard_map(body, mesh=mesh, in_specs=in_specs, out_specs=out_specs, check_vma=False)
```

profile of v0, /device:TPU:1, one launch (start us, length us, event | category | flops | bytes accessed | tf_op | source)
XLA Modules:
  0.0 328.8 jit_solution(11202653416886925605)
XLA Ops:
  6.5 1.5 copy.41
  8.1 2.9 copy.40
  11.0 64.0 %all-gather.2.cloned.1.call-done = bf16[8,1024,128]{2,0,1:T(8,128)(2,1)} async-done(((bf16[8,32,128]{2,0,1:T(8,128)(2,1)}), bf16[8,1024,128]{2,0,1:T(8,128)(2,1)}) %all-gather.2.cloned.1.call-update) | async-done | bytes 2097168 | tf_op jit(solution)/shard_map/all_gather | solution.py:35
  75.1 4.3 %fusion.93 = (bf16[8,1024,64]{2,0,1:T(8,128)(2,1)}, bf16[8,1024,64]{2,0,1:T(8,128)(2,1)S(1)}) fusion(bf16[8,1024,128]{2,0,1:T(8,128)(2,1)} %all-gather.2.cloned.1.call-done), kind=kLoop, calls=%fused_computation.149 | loop fusion | bytes 4194304 | tf_op jit(solution)/shard_map/slice | solution.py:39
  79.4 0.8 fusion
  80.1 2.2 fusion.12
  82.3 2.5 copy.88
  84.9 1.6 fusion.38
  86.5 1.6 fusion.8
  88.1 0.7 copy-done.2
  88.8 1.0 select_reduce_fusion.5
  90.5 5.8 %cholesky.89 = f32[64,64]{1,0:T(8,128)S(1)} custom-call(f32[64,64]{1,0:T(8,128)S(1)} %fusion.68), custom_call_target="Cholesky" | custom-call | tf_op jit(solution)/shard_map/jit(cholesky)/cholesky | solution.py:19
  96.4 0.6 compare_reduce_fusion.4
  97.1 0.7 fusion.49
  97.7 4.9 %custom-call.9 = f32[1,64,64]{1,2,0:T(8,128)S(1)} custom-call(f32[1,64,64]{2,1,0:T(8,128)S(1)} %fusion.49), custom_call_target="InvertDiagBlocksLowerTriangular" | custom-call | tf_op jit(solution)/shard_map/triangular_solve/custom-call.0 | solution.py:20
  102.6 1.4 fusion.66
  104.0 3.2 fusion.2
  107.2 0.7 convolution_bitcast_fusion.8
  108.0 3.4 %collective-permute-start = (f32[1024,128]{0,1:T(8,128)S(1)}, f32[1024,128]{0,1:T(8,128)S(1)}, u32[]{:S(2)}, u32[]{:S(2)}) collective-permute-start(f32[1024,128]{0,1:T(8,128)S(1)} %pad_maximum_fusion.4), channel_id=1, source_target_pairs={{0,1},{1,0},{2,3},{3,2},{4,5},{5,4},{6,7},{7,6},{8,9},{9,8},{10,11... | collective-permute-start | bytes 1572872 | tf_op jit(solution)/shard_map/ppermute | solution.py:8
  111.4 11.7 %collective-permute-done = f32[1024,128]{0,1:T(8,128)S(1)} collective-permute-done((f32[1024,128]{0,1:T(8,128)S(1)}, f32[1024,128]{0,1:T(8,128)S(1)}, u32[]{:S(2)}, u32[]{:S(2)}) %collective-permute-start) | collective-permute-done | bytes 524320 | tf_op jit(solution)/shard_map/ppermute | solution.py:8
  123.1 1.1 select_bitcast_fusion.7
  124.2 0.9 fusion.36
  125.0 0.4 convolution_bitcast_fusion.7
  125.5 1.0 select_reduce_fusion.4
  127.2 5.8 %cholesky.100 = f32[64,64]{1,0:T(8,128)S(1)} custom-call(f32[64,64]{1,0:T(8,128)S(1)} %fusion.65), custom_call_target="Cholesky" | custom-call | tf_op jit(solution)/shard_map/jit(cholesky)/cholesky | solution.py:19
  133.1 0.6 compare_reduce_fusion.3
  133.8 0.7 fusion.50
  134.4 4.9 %custom-call.10 = f32[1,64,64]{1,2,0:T(8,128)S(1)} custom-call(f32[1,64,64]{2,1,0:T(8,128)S(1)} %fusion.50), custom_call_target="InvertDiagBlocksLowerTriangular" | custom-call | tf_op jit(solution)/shard_map/triangular_solve/custom-call.0 | solution.py:20
  139.7 0.9 fusion.27
  140.6 0.4 convolution_bitcast_fusion.6
  141.1 4.2 %collective-permute-start.1 = (f32[1024,128]{0,1:T(8,128)S(1)}, f32[1024,128]{0,1:T(8,128)S(1)}, u32[]{:S(2)}, u32[]{:S(2)}) collective-permute-start(f32[1024,128]{0,1:T(8,128)S(1)} %pad_maximum_fusion.5), channel_id=1, source_target_pairs={{0,2},{1,3},{2,0},{3,1},{4,6},{5,7},{6,4},{7,5},{8,10},{9,11},{10,... | collective-permute-start | bytes 1572872 | tf_op jit(solution)/shard_map/ppermute | solution.py:8
  145.3 22.7 %collective-permute-done.1 = f32[1024,128]{0,1:T(8,128)S(1)} collective-permute-done((f32[1024,128]{0,1:T(8,128)S(1)}, f32[1024,128]{0,1:T(8,128)S(1)}, u32[]{:S(2)}, u32[]{:S(2)}) %collective-permute-start.1) | collective-permute-done | bytes 524320 | tf_op jit(solution)/shard_map/ppermute | solution.py:8
  168.1 0.9 fusion.34
  169.0 0.4 convolution_bitcast_fusion.5
  169.4 1.0 select_reduce_fusion.3
  171.2 5.8 %cholesky.111 = f32[64,64]{1,0:T(8,128)S(1)} custom-call(f32[64,64]{1,0:T(8,128)S(1)} %fusion.62), custom_call_target="Cholesky" | custom-call | tf_op jit(solution)/shard_map/jit(cholesky)/cholesky | solution.py:19
  177.1 0.6 compare_reduce_fusion.2
  177.7 0.7 fusion.51
  178.4 4.9 %custom-call.11 = f32[1,64,64]{1,2,0:T(8,128)S(1)} custom-call(f32[1,64,64]{2,1,0:T(8,128)S(1)} %fusion.51), custom_call_target="InvertDiagBlocksLowerTriangular" | custom-call | tf_op jit(solution)/shard_map/triangular_solve/custom-call.0 | solution.py:20
  183.7 0.9 fusion.25
  184.6 0.4 convolution_bitcast_fusion.4
  185.1 7.6 %collective-permute-start.2 = (f32[1024,128]{0,1:T(8,128)S(1)}, f32[1024,128]{0,1:T(8,128)S(1)}, u32[]{:S(2)}, u32[]{:S(2)}) collective-permute-start(f32[1024,128]{0,1:T(8,128)S(1)} %pad_maximum_fusion.6), channel_id=1, source_target_pairs={{0,4},{1,5},{2,6},{3,7},{4,0},{5,1},{6,2},{7,3},{8,12},{9,13},{10,... | collective-permute-start | bytes 1572872 | tf_op jit(solution)/shard_map/ppermute | solution.py:8
  192.7 44.8 %collective-permute-done.2 = f32[1024,128]{0,1:T(8,128)S(1)} collective-permute-done((f32[1024,128]{0,1:T(8,128)S(1)}, f32[1024,128]{0,1:T(8,128)S(1)}, u32[]{:S(2)}, u32[]{:S(2)}) %collective-permute-start.2) | collective-permute-done | bytes 524320 | tf_op jit(solution)/shard_map/ppermute | solution.py:8
  237.6 0.9 fusion.32
  238.5 0.4 convolution_bitcast_fusion.3
  239.0 1.0 select_reduce_fusion.2
  240.7 5.8 %cholesky.122 = f32[64,64]{1,0:T(8,128)S(1)} custom-call(f32[64,64]{1,0:T(8,128)S(1)} %fusion.59), custom_call_target="Cholesky" | custom-call | tf_op jit(solution)/shard_map/jit(cholesky)/cholesky | solution.py:19
  246.6 0.6 compare_reduce_fusion.1
  247.2 0.7 fusion.52
  247.9 4.9 %custom-call.12 = f32[1,64,64]{1,2,0:T(8,128)S(1)} custom-call(f32[1,64,64]{2,1,0:T(8,128)S(1)} %fusion.52), custom_call_target="InvertDiagBlocksLowerTriangular" | custom-call | tf_op jit(solution)/shard_map/triangular_solve/custom-call.0 | solution.py:20
  253.2 0.9 fusion.23
  254.1 0.4 convolution_bitcast_fusion.2
  254.6 11.1 %collective-permute-start.3 = (f32[1024,128]{0,1:T(8,128)S(1)}, f32[1024,128]{0,1:T(8,128)S(1)}, u32[]{:S(2)}, u32[]{:S(2)}) collective-permute-start(f32[1024,128]{0,1:T(8,128)S(1)} %pad_maximum_fusion.7), channel_id=1, source_target_pairs={{0,8},{1,9},{2,10},{3,11},{4,12},{5,13},{6,14},{7,15},{8,0},{9,1},... | collective-permute-start | bytes 1572872 | tf_op jit(solution)/shard_map/ppermute | solution.py:8
  265.7 38.4 %collective-permute-done.3 = f32[1024,128]{0,1:T(8,128)S(1)} collective-permute-done((f32[1024,128]{0,1:T(8,128)S(1)}, f32[1024,128]{0,1:T(8,128)S(1)}, u32[]{:S(2)}, u32[]{:S(2)}) %collective-permute-start.3) | collective-permute-done | bytes 524320 | tf_op jit(solution)/shard_map/ppermute | solution.py:8
  304.2 0.9 fusion.30
  305.1 0.4 convolution_bitcast_fusion.1
  305.6 1.0 select_reduce_fusion.1
  307.3 5.8 %cholesky.133 = f32[64,64]{1,0:T(8,128)S(1)} custom-call(f32[64,64]{1,0:T(8,128)S(1)} %fusion.56), custom_call_target="Cholesky" | custom-call | tf_op jit(solution)/shard_map/jit(cholesky)/cholesky | solution.py:19
  313.2 0.6 compare_reduce_fusion
  313.8 0.7 fusion.53
  314.5 4.9 %custom-call.13 = f32[1,64,64]{1,2,0:T(8,128)S(1)} custom-call(f32[1,64,64]{2,1,0:T(8,128)S(1)} %fusion.53), custom_call_target="InvertDiagBlocksLowerTriangular" | custom-call | tf_op jit(solution)/shard_map/triangular_solve/custom-call.0 | solution.py:20
  319.8 0.9 fusion.21
  320.7 0.4 fusion.11
  321.2 0.7 copy.70
  (44 shorter events, 3.0 us)
Async XLA Ops:
  6.5 78.3 %copy-start = (f32[64,1024]{1,0:T(8,128)S(1)}, f32[64,1024]{1,0:T(8,128)}, u32[]{:S(2)}) copy-start(f32[64,1024]{1,0:T(8,128)} %param.10) | copy-start | bytes 786436
  6.5 68.5 %all-gather.2.cloned.1.call-start = ((), (), s32[]{:S(2)}) async-start(), calls=%async_computation | async-start | bytes 2162688 | tf_op jit(solution)/shard_map/all_gather | solution.py:35
  8.1 2.9 copy-start.4
  11.0 68.4 %copy-start.1 = (bf16[1,8,1024,128]{2,3,1,0:T(8,128)(2,1)}, bf16[1,8,1024,128]{2,3,1,0:T(8,128)(2,1)S(1)}, u32[]{:S(2)}) copy-start(bf16[1,8,1024,128]{2,3,1,0:T(8,128)(2,1)S(1)} %copy.40) | copy-start | bytes 6291460
  88.1 0.7 copy-start.2
  104.0 4.0 %copy-start.3 = (f32[64,1024]{1,0:T(8,128)}, f32[64,1024]{1,0:T(8,128)S(1)}, u32[]{:S(2)}) copy-start(f32[64,1024]{1,0:T(8,128)S(1)} %fusion.66) | copy-start | bytes 786436
  108.0 15.1 %collective-permute-start = (f32[1024,128]{0,1:T(8,128)S(1)}, f32[1024,128]{0,1:T(8,128)S(1)}, u32[]{:S(2)}, u32[]{:S(2)}) collective-permute-start(f32[1024,128]{0,1:T(8,128)S(1)} %pad_maximum_fusion.4), channel_id=1, source_target_pairs={{0,1},{1,0},{2,3},{3,2},{4,5},{5,4},{6,7},{7,6},{8,9},{9,8},{10,11... | collective-permute-start | bytes 1572872 | tf_op jit(solution)/shard_map/ppermute | solution.py:8
  141.1 26.9 %collective-permute-start.1 = (f32[1024,128]{0,1:T(8,128)S(1)}, f32[1024,128]{0,1:T(8,128)S(1)}, u32[]{:S(2)}, u32[]{:S(2)}) collective-permute-start(f32[1024,128]{0,1:T(8,128)S(1)} %pad_maximum_fusion.5), channel_id=1, source_target_pairs={{0,2},{1,3},{2,0},{3,1},{4,6},{5,7},{6,4},{7,5},{8,10},{9,11},{10,... | collective-permute-start | bytes 1572872 | tf_op jit(solution)/shard_map/ppermute | solution.py:8
  185.1 52.5 %collective-permute-start.2 = (f32[1024,128]{0,1:T(8,128)S(1)}, f32[1024,128]{0,1:T(8,128)S(1)}, u32[]{:S(2)}, u32[]{:S(2)}) collective-permute-start(f32[1024,128]{0,1:T(8,128)S(1)} %pad_maximum_fusion.6), channel_id=1, source_target_pairs={{0,4},{1,5},{2,6},{3,7},{4,0},{5,1},{6,2},{7,3},{8,12},{9,13},{10,... | collective-permute-start | bytes 1572872 | tf_op jit(solution)/shard_map/ppermute | solution.py:8
  254.6 49.5 %collective-permute-start.3 = (f32[1024,128]{0,1:T(8,128)S(1)}, f32[1024,128]{0,1:T(8,128)S(1)}, u32[]{:S(2)}, u32[]{:S(2)}) collective-permute-start(f32[1024,128]{0,1:T(8,128)S(1)} %pad_maximum_fusion.7), channel_id=1, source_target_pairs={{0,8},{1,9},{2,10},{3,11},{4,12},{5,13},{6,14},{7,15},{8,0},{9,1},... | collective-permute-start | bytes 1572872 | tf_op jit(solution)/shard_map/ppermute | solution.py:8
Sparse Core Ops, SparseCore 0:
  10.5 64.5 all-gather.1
where the time goes:
time: 329 us
  waiting for transfers between devices  182 us (55%)
  other arithmetic  62.1 us (19%)
  matrix products  28.6 us (9%)
  starting transfers between devices  26.3 us (8%)
  between operations  17.1 us (5%)
  local copies, waits for them, and re-layouts  13 us (4%)
    ppermute x4, waiting for transfers between devices, from_partner(): lax.ppermute(shard, axis, [(i, i ^ 1 << stride) for i in range(lax.axis_s...  118 us
    all_gather x1, waiting for transfers between devices, body(): panel = lax.all_gather(panel_factors, 'rows', axis=1, tiled=True)  64 us
    another operation x15, other arithmetic, compress(): chol = jnp.linalg.cholesky(gram)  32.6 us
    another operation x10, other arithmetic, compress(): lax.linalg.triangular_solve(chol, span, left_side=False, lower=True, tran...  27.7 us
    ppermute x4, starting transfers between devices, from_partner(): lax.ppermute(shard, axis, [(i, i ^ 1 << stride) for i in range(lax.axis_s...  26.3 us
    unnamed x13, local copies, waits for them, and re-layouts  7.62 us
    dot_general x5, matrix products, compress(): coef = jnp.einsum('nbr,bs->nrs', lefts, basis, precision=hi)  6.75 us
  transfers between devices with their start and end apart: 5, of which 5 were waited for; matrix products, arithmetic and copies ran while one was open for 1% of the time, Pallas kernels for 0%

commit v1 on v0

--- a/solution.py
+++ b/solution.py
@@ -2,6 +2,13 @@
 import jax.numpy as jnp
 from jax import lax
 from jax.sharding import PartitionSpec as P
+
+
+def all_by_exchange(array, axis, along):
+    count = lax.axis_size(axis)
+    tiles = jnp.stack([array for _ in range(count)])
+    tiles = lax.all_to_all(tiles, axis, split_axis=0, concat_axis=0)
+    return jnp.concatenate(tiles, axis=along)
 
 
 def from_partner(shard, axis, stride):
@@ -32,7 +39,7 @@
     rank = tile_factors.shape[3] // 2
     tiles = tile_factors[0]
     own_right = tiles[:, :, rank:]
-    panel = lax.all_gather(panel_factors, "rows", axis=1, tiled=True)
+    panel = all_by_exchange(panel_factors, "rows", 1)
     inner = jnp.einsum(
         "kbr,kbs->krs", own_right, panel[:, :, rank:], preferred_element_type=jnp.float32
     )

time: 329 us -> 287 us (0.87)
  waiting for transfers between devices: 182 us -> 148 us
  between operations: 17.1 us -> 3.73 us
  starting transfers between devices: 26.3 us -> 34.4 us
  local copies, waits for them, and re-layouts: 13 us -> 8.57 us
    all_gather x1 -> x0, waiting for transfers between devices: 64 us -> none  [body(): panel = lax.all_gather(panel_factors, 'rows', axis=1, tiled=True)]
    all_to_all x0 -> x1, waiting for transfers between devices: none -> 25.8 us  [all_by_exchange(): tiles = lax.all_to_all(tiles, axis, split_axis=0, concat_axis=0)]
    all_to_all x0 -> x1, starting transfers between devices: none -> 11.3 us  [all_by_exchange(): tiles = lax.all_to_all(tiles, axis, split_axis=0, concat_axis=0)]
    unnamed x13 -> x11, local copies, waits for them, and re-layouts: 7.62 us -> 2.67 us
    ppermute x4, waiting for transfers between devices: 118 us -> 123 us  [from_partner(): lax.ppermute(shard, axis, [(i, i ^ 1 << stride) for i in range(lax.axis_s...]
    slice x1 -> x0, local copies, waits for them, and re-layouts: 4.28 us -> none  [body(): far_left = panel[:, :, :rank]]
where the time goes in v1:
time: 287 us; the launch traced here: 286 us
  waiting for transfers between devices  148 us (52%)
  other arithmetic  61.2 us (21%)
  starting transfers between devices  34.4 us (12%)
  matrix products  29.9 us (10%)
  local copies, waits for them, and re-layouts  8.57 us (3%)
  between operations  3.73 us (1%)
    ppermute x4, waiting for transfers between devices, from_partner(): lax.ppermute(shard, axis, [(i, i ^ 1 << stride) for i in range(lax.axis_s...  123 us
    another operation x15, other arithmetic, compress(): chol = jnp.linalg.cholesky(gram)  32.6 us
    another operation x10, other arithmetic, compress(): lax.linalg.triangular_solve(chol, span, left_side=False, lower=True, tran...  27.7 us
    all_to_all x1, waiting for transfers between devices, all_by_exchange(): tiles = lax.all_to_all(tiles, axis, split_axis=0, concat_axis=0)  25.8 us
    ppermute x4, starting transfers between devices, from_partner(): lax.ppermute(shard, axis, [(i, i ^ 1 << stride) for i in range(lax.axis_s...  23.1 us
    all_to_all x1, starting transfers between devices, all_by_exchange(): tiles = lax.all_to_all(tiles, axis, split_axis=0, concat_axis=0)  11.3 us
    dot_general x5, matrix products, compress(): coef = jnp.einsum('nbr,bs->nrs', lefts, basis, precision=hi)  8.34 us
  transfers between devices with their start and end apart: 5, of which 5 were waited for; matrix products, arithmetic and copies ran while one was open for 1% of the time, Pallas kernels for 0%

profile of v1, /device:TPU:1, one launch (start us, length us, event | category | flops | bytes accessed | tf_op | source)
XLA Modules:
  0.0 286.2 jit_solution(6937100170455171208)
XLA Ops:
  0.0 2.6 stack.26
  2.7 11.3 %all-to-all-start = ((bf16[32,8,32,128]{3,2,1,0:T(8,128)(2,1)}), bf16[32,8,32,128]{3,2,1,0:T(8,128)(2,1)}, u32[]{:S(2)}, u32[]{:S(2)}) async-start(bf16[32,8,32,128]{3,2,1,0:T(8,128)(2,1)} %stack.26), calls=%async_computation | async-start | bytes 4194304 | tf_op jit(solution)/shard_map/all_to_all | solution.py:10
  14.0 2.6 copy.40
  16.6 25.8 %all-to-all-done = bf16[32,8,32,128]{3,2,1,0:T(8,128)(2,1)} async-done(((bf16[32,8,32,128]{3,2,1,0:T(8,128)(2,1)}), bf16[32,8,32,128]{3,2,1,0:T(8,128)(2,1)}, u32[]{:S(2)}, u32[]{:S(2)}) %all-to-all-start) | async-done | bytes 2097184 | tf_op jit(solution)/shard_map/all_to_all | solution.py:10
  42.5 2.2 copy.41
  44.7 1.8 fusion
  46.5 1.0 fusion.19
  47.5 1.2 fusion.8
  48.7 1.6 fusion.15
  50.3 1.0 select_reduce_fusion.5
  52.1 5.8 %cholesky.89 = f32[64,64]{1,0:T(8,128)S(1)} custom-call(f32[64,64]{1,0:T(8,128)S(1)} %fusion.74), custom_call_target="Cholesky" | custom-call | tf_op jit(solution)/shard_map/jit(cholesky)/cholesky | solution.py:26
  57.9 0.6 compare_reduce_fusion.4
  58.6 0.7 fusion.55
  59.3 4.9 %custom-call.9 = f32[1,64,64]{1,2,0:T(8,128)S(1)} custom-call(f32[1,64,64]{2,1,0:T(8,128)S(1)} %fusion.55), custom_call_target="InvertDiagBlocksLowerTriangular" | custom-call | tf_op jit(solution)/shard_map/triangular_solve/custom-call.0 | solution.py:27
  64.6 4.8 %fusion.2 = f32[8,64,64]{1,2,0:T(8,128)S(1)} fusion(f32[8,64,1024]{2,1,0:T(8,128)} %copy-done.1, f32[8]{0:T(128)S(1)} %convert_bitcast_fusion, f32[64,1024]{1,0:T(8,128)S(1)} %fusion.72), kind=kOutput, calls=%fused_computation.2 | convolution fusion | flops 403177472 | bytes 2490400 | tf_op jit(solution)/shard_map/nbr,bs->nrs/dot_general | solution.py:28
  69.4 2.0 fusion.12
  71.5 2.1 collective-permute-start
  73.6 12.4 %collective-permute-done = f32[1024,128]{0,1:T(8,128)S(1)} collective-permute-done((f32[1024,128]{0,1:T(8,128)S(1)}, f32[1024,128]{0,1:T(8,128)S(1)}, u32[]{:S(2)}, u32[]{:S(2)}) %collective-permute-start) | collective-permute-done | bytes 524320 | tf_op jit(solution)/shard_map/ppermute | solution.py:15
  86.1 0.9 fusion.43
  87.0 0.4 convolution_bitcast_fusion.7
  87.5 1.0 select_reduce_fusion.4
  89.2 5.8 %cholesky.100 = f32[64,64]{1,0:T(8,128)S(1)} custom-call(f32[64,64]{1,0:T(8,128)S(1)} %fusion.71), custom_call_target="Cholesky" | custom-call | tf_op jit(solution)/shard_map/jit(cholesky)/cholesky | solution.py:26
  95.1 0.6 compare_reduce_fusion.3
  95.7 0.7 fusion.56
  96.4 4.9 %custom-call.10 = f32[1,64,64]{1,2,0:T(8,128)S(1)} custom-call(f32[1,64,64]{2,1,0:T(8,128)S(1)} %fusion.56), custom_call_target="InvertDiagBlocksLowerTriangular" | custom-call | tf_op jit(solution)/shard_map/triangular_solve/custom-call.0 | solution.py:27
  101.7 0.9 fusion.34
  102.6 0.4 convolution_bitcast_fusion.6
  103.1 2.6 collective-permute-start.1
  105.7 25.2 %collective-permute-done.1 = f32[1024,128]{0,1:T(8,128)S(1)} collective-permute-done((f32[1024,128]{0,1:T(8,128)S(1)}, f32[1024,128]{0,1:T(8,128)S(1)}, u32[]{:S(2)}, u32[]{:S(2)}) %collective-permute-start.1) | collective-permute-done | bytes 524320 | tf_op jit(solution)/shard_map/ppermute | solution.py:15
  131.1 0.9 fusion.41
  132.0 0.4 convolution_bitcast_fusion.5
  132.4 1.0 select_reduce_fusion.3
  134.1 5.8 %cholesky.111 = f32[64,64]{1,0:T(8,128)S(1)} custom-call(f32[64,64]{1,0:T(8,128)S(1)} %fusion.68), custom_call_target="Cholesky" | custom-call | tf_op jit(solution)/shard_map/jit(cholesky)/cholesky | solution.py:26
  140.0 0.6 compare_reduce_fusion.2
  140.7 0.7 fusion.57
  141.3 4.9 %custom-call.11 = f32[1,64,64]{1,2,0:T(8,128)S(1)} custom-call(f32[1,64,64]{2,1,0:T(8,128)S(1)} %fusion.57), custom_call_target="InvertDiagBlocksLowerTriangular" | custom-call | tf_op jit(solution)/shard_map/triangular_solve/custom-call.0 | solution.py:27
  146.2 0.4 fusion.66
  146.7 0.9 fusion.32
  147.5 0.4 convolution_bitcast_fusion.4
  148.0 6.4 %collective-permute-start.2 = (f32[1024,128]{0,1:T(8,128)S(1)}, f32[1024,128]{0,1:T(8,128)S(1)}, u32[]{:S(2)}, u32[]{:S(2)}) collective-permute-start(f32[1024,128]{0,1:T(8,128)S(1)} %pad_maximum_fusion.6), channel_id=1, source_target_pairs={{0,4},{1,5},{2,6},{3,7},{4,0},{5,1},{6,2},{7,3},{8,12},{9,13},{10,... | collective-permute-start | bytes 1572872 | tf_op jit(solution)/shard_map/ppermute | solution.py:15
  154.5 45.9 %collective-permute-done.2 = f32[1024,128]{0,1:T(8,128)S(1)} collective-permute-done((f32[1024,128]{0,1:T(8,128)S(1)}, f32[1024,128]{0,1:T(8,128)S(1)}, u32[]{:S(2)}, u32[]{:S(2)}) %collective-permute-start.2) | collective-permute-done | bytes 524320 | tf_op jit(solution)/shard_map/ppermute | solution.py:15
  200.5 0.9 fusion.39
  201.4 0.4 convolution_bitcast_fusion.3
  201.8 1.0 select_reduce_fusion.2
  203.6 5.8 %cholesky.122 = f32[64,64]{1,0:T(8,128)S(1)} custom-call(f32[64,64]{1,0:T(8,128)S(1)} %fusion.65), custom_call_target="Cholesky" | custom-call | tf_op jit(solution)/shard_map/jit(cholesky)/cholesky | solution.py:26
  209.4 0.6 compare_reduce_fusion.1
  210.1 0.7 fusion.58
  210.7 4.9 %custom-call.12 = f32[1,64,64]{1,2,0:T(8,128)S(1)} custom-call(f32[1,64,64]{2,1,0:T(8,128)S(1)} %fusion.58), custom_call_target="InvertDiagBlocksLowerTriangular" | custom-call | tf_op jit(solution)/shard_map/triangular_solve/custom-call.0 | solution.py:27
  215.6 0.4 fusion.63
  216.1 0.9 fusion.30
  216.9 0.4 convolution_bitcast_fusion.2
  217.4 12.0 %collective-permute-start.3 = (f32[1024,128]{0,1:T(8,128)S(1)}, f32[1024,128]{0,1:T(8,128)S(1)}, u32[]{:S(2)}, u32[]{:S(2)}) collective-permute-start(f32[1024,128]{0,1:T(8,128)S(1)} %pad_maximum_fusion.7), channel_id=1, source_target_pairs={{0,8},{1,9},{2,10},{3,11},{4,12},{5,13},{6,14},{7,15},{8,0},{9,1},... | collective-permute-start | bytes 1572872 | tf_op jit(solution)/shard_map/ppermute | solution.py:15
  229.4 39.0 %collective-permute-done.3 = f32[1024,128]{0,1:T(8,128)S(1)} collective-permute-done((f32[1024,128]{0,1:T(8,128)S(1)}, f32[1024,128]{0,1:T(8,128)S(1)}, u32[]{:S(2)}, u32[]{:S(2)}) %collective-permute-start.3) | collective-permute-done | bytes 524320 | tf_op jit(solution)/shard_map/ppermute | solution.py:15
  268.5 0.9 fusion.37
  269.4 0.4 convolution_bitcast_fusion.1
  269.8 1.0 select_reduce_fusion.1
  271.6 5.8 %cholesky.133 = f32[64,64]{1,0:T(8,128)S(1)} custom-call(f32[64,64]{1,0:T(8,128)S(1)} %fusion.62), custom_call_target="Cholesky" | custom-call | tf_op jit(solution)/shard_map/jit(cholesky)/cholesky | solution.py:26
  277.4 0.6 compare_reduce_fusion
  278.1 0.7 fusion.59
  278.7 4.9 %custom-call.13 = f32[1,64,64]{1,2,0:T(8,128)S(1)} custom-call(f32[1,64,64]{2,1,0:T(8,128)S(1)} %fusion.59), custom_call_target="InvertDiagBlocksLowerTriangular" | custom-call | tf_op jit(solution)/shard_map/triangular_solve/custom-call.0 | solution.py:27
  283.6 0.4 bitcast_multiply_fusion
  284.1 0.9 fusion.28
  285.0 0.4 fusion.18
  285.5 0.7 copy.70
  (42 shorter events, 2.3 us)
Async XLA Ops:
  0.0 47.5 %copy-start = (f32[64,1024]{1,0:T(8,128)S(1)}, f32[64,1024]{1,0:T(8,128)}, u32[]{:S(2)}) copy-start(f32[64,1024]{1,0:T(8,128)} %param.10) | copy-start | bytes 786436
  2.7 11.3 %copy-start.3 = (bf16[1,8,1024,128]{3,2,1,0:T(8,128)(2,1)S(1)}, bf16[1,8,1024,128]{3,2,1,0:T(8,128)(2,1)}, u32[]{:S(2)}) copy-start(bf16[1,8,1024,128]{3,2,1,0:T(8,128)(2,1)} %param.7) | copy-start | bytes 6291460
  2.7 39.8 %all-to-all-start = ((bf16[32,8,32,128]{3,2,1,0:T(8,128)(2,1)}), bf16[32,8,32,128]{3,2,1,0:T(8,128)(2,1)}, u32[]{:S(2)}, u32[]{:S(2)}) async-start(bf16[32,8,32,128]{3,2,1,0:T(8,128)(2,1)} %stack.26), calls=%async_computation | async-start | bytes 4194304 | tf_op jit(solution)/shard_map/all_to_all | solution.py:10
  14.0 2.6 copy-start.4
  42.4 2.2 copy-start.2
  47.5 2.8 copy-start.1
  71.5 14.6 %collective-permute-start = (f32[1024,128]{0,1:T(8,128)S(1)}, f32[1024,128]{0,1:T(8,128)S(1)}, u32[]{:S(2)}, u32[]{:S(2)}) collective-permute-start(f32[1024,128]{0,1:T(8,128)S(1)} %pad_maximum_fusion.4), channel_id=1, source_target_pairs={{0,1},{1,0},{2,3},{3,2},{4,5},{5,4},{6,7},{7,6},{8,9},{9,8},{10,11... | collective-permute-start | bytes 1572872 | tf_op jit(solution)/shard_map/ppermute | solution.py:15
  103.1 27.9 %collective-permute-start.1 = (f32[1024,128]{0,1:T(8,128)S(1)}, f32[1024,128]{0,1:T(8,128)S(1)}, u32[]{:S(2)}, u32[]{:S(2)}) collective-permute-start(f32[1024,128]{0,1:T(8,128)S(1)} %pad_maximum_fusion.5), channel_id=1, source_target_pairs={{0,2},{1,3},{2,0},{3,1},{4,6},{5,7},{6,4},{7,5},{8,10},{9,11},{10,... | collective-permute-start | bytes 1572872 | tf_op jit(solution)/shard_map/ppermute | solution.py:15
  148.0 52.3 %collective-permute-start.2 = (f32[1024,128]{0,1:T(8,128)S(1)}, f32[1024,128]{0,1:T(8,128)S(1)}, u32[]{:S(2)}, u32[]{:S(2)}) collective-permute-start(f32[1024,128]{0,1:T(8,128)S(1)} %pad_maximum_fusion.6), channel_id=1, source_target_pairs={{0,4},{1,5},{2,6},{3,7},{4,0},{5,1},{6,2},{7,3},{8,12},{9,13},{10,... | collective-permute-start | bytes 1572872 | tf_op jit(solution)/shard_map/ppermute | solution.py:15
  217.4 50.9 %collective-permute-start.3 = (f32[1024,128]{0,1:T(8,128)S(1)}, f32[1024,128]{0,1:T(8,128)S(1)}, u32[]{:S(2)}, u32[]{:S(2)}) collective-permute-start(f32[1024,128]{0,1:T(8,128)S(1)} %pad_maximum_fusion.7), channel_id=1, source_target_pairs={{0,8},{1,9},{2,10},{3,11},{4,12},{5,13},{6,14},{7,15},{8,0},{9,1},... | collective-permute-start | bytes 1572872 | tf_op jit(solution)/shard_map/ppermute | solution.py:15
